TPU v7x, 256 devices: a whole 4x4x8 slice. The times are simulated.
256 devices in a mesh: order: 64 (over z, x, core), lat: 4 (over y).
Axes of the slice: x: 4, y: 4, z: 8, core: 2. Of those that a mesh axis runs over, the one named last changes fastest.
Arguments:
- position: float32 [128, 2, 64, 2160], P('order', None, None, 'lat'), may hold values from -6 to 6
- residual: float32 [128, 2, 64, 2160], P('order', None, None, 'lat'), as said below
- direction: float32 [128, 2, 64, 2160], P('order', None, None, 'lat'), as said below
- legendre: float32 [128, 2160, 2048], P('order', None, 'lat'), may hold values from -0.125 to 0.125
- order_of: int32 [128], replicated, may hold values from 0 to 2032, as said below
- class_idx: int32 [2048, 4320], P(('lat', 'order')), may hold values from 0 to 15
- land: int32 [2048, 4320], P(('lat', 'order')), may hold values 0 or 1
- class_weight: float32 [16, 2], replicated, may hold values from 0.2 to 5
- damping: float32 [2160], P('lat'), may hold values from 0.05 to 0.5
Outputs:
- new_position: float32 [128, 2, 64, 2160], P('order', None, None, 'lat')
- new_residual: float32 [128, 2, 64, 2160], P('order', None, None, 'lat')
- new_direction: float32 [128, 2, 64, 2160], P('order', None, None, 'lat')
Inputs may be any that keep to these rules, and one draw needn't show every extreme that they name: `order_of`: distinct multiples of 16: each of 0, 16, ..., 16 * (128 - 1) appears exactly once. `residual`: real-valued and not zero. `direction`: real-valued and not zero.
All inputs are finite; a program needn't handle non-finite values. No bound on the sum of `land` on one device may be relied on, other than what follows from the above.
Results may differ from a plain program's by a relative error of at most 0.000058.
Values sent between devices are 32-bit elements; how exact they have to be, the bound alone decides.
A program may use at most 128 MiB of HBM per device.

v0:
```python
import math
import jax
import jax.numpy as jnp
from jax import lax
from jax.sharding import PartitionSpec as P


def tables(order_of, longitudes):
    longitude = jnp.arange(longitudes, dtype=jnp.int32)
    phases = order_of[:, None] * longitude[None, :] % longitudes
    angles = phases.astype(jnp.float32) * (2.0 * math.pi / longitudes)
    return jnp.stack([jnp.cos(angles), jnp.sin(angles)])


def sample_sums(product):
    return jnp.sum(product, axis=(0, 1, 3))


def shards(
    position, residual, direction, legendre, order_of, class_idx, land, class_weight, damping
):
    highest = lax.Precision.HIGHEST
    m_local = position.shape[0]
    samples = position.shape[2]
    deg_local = position.shape[3]
    band_rows = legendre.shape[2]
    lat_index = lax.axis_index("lat")
    order_index = lax.axis_index("order")
    my_orders = lax.dynamic_slice_in_dim(order_of, order_index * m_local, m_local)
    deg_start = lat_index * deg_local
    own_degrees = deg_start + jnp.arange(deg_local, dtype=jnp.int32)
    own_valid = (own_degrees[None, :] >= my_orders[:, None]).astype(jnp.float32)[:, None, None, :]
    pos_m = position * own_valid
    res_m = residual * own_valid
    dir_m = direction * own_valid
    norm_before = lax.psum(sample_sums(res_m * res_m), ("order", "lat"))
    block_part = lax.all_gather(direction, "lat", axis=3, tiled=True)
    degree_count = block_part.shape[3]
    in_block = jnp.arange(degree_count, dtype=jnp.int32)
    in_triangle = (in_block[None, :] >= my_orders[:, None]).astype(jnp.float32)
    masked = block_part * in_triangle[:, None, None, :]
    synthesis = jnp.einsum("mskd,mdt->mtsk", masked, legendre, precision=highest)
    grid_in = lax.all_to_all(
        synthesis.reshape(m_local, band_rows, 2 * samples),
        "order",
        split_axis=1,
        concat_axis=0,
        tiled=True,
    )
    orders_all = grid_in.shape[0]
    rows_here = grid_in.shape[1]
    grid_in = grid_in.reshape(orders_all, rows_here, 2, samples)
    longitudes = class_idx.shape[1]
    harmonic = tables(order_of, longitudes)
    surface = jnp.einsum("mrsk,sml->rkl", grid_in, harmonic, precision=highest)
    class_count = class_weight.shape[0]
    onehot = (
        class_idx[:, :, None] == jnp.arange(class_count, dtype=jnp.int32)[None, None, :]
    ).astype(jnp.float32)
    by_class = jnp.dot(onehot, class_weight, precision=highest)
    weight_grid = jnp.where(land == 1, by_class[:, :, 1], by_class[:, :, 0])
    weighted = surface * weight_grid[:, None, :]
    spectra = jnp.einsum("rkl,sml->mrsk", weighted, harmonic, precision=highest) * (
        2.0 / longitudes
    )
    returned = lax.all_to_all(
        spectra.reshape(orders_all, rows_here, 2 * samples),
        "order",
        split_axis=0,
        concat_axis=1,
        tiled=True,
    )
    returned = returned.reshape(m_local, band_rows, 2, samples)
    band_part = jnp.einsum("mtsk,mdt->mskd", returned, legendre, precision=highest)
    totals = lax.psum(band_part, "lat")
    summed = lax.dynamic_slice_in_dim(totals, deg_start, deg_local, 3)
    applied = (summed + damping[None, None, None, :] * dir_m) * own_valid
    curvature_sum = lax.psum(sample_sums(dir_m * applied), ("order", "lat"))
    step_size = (norm_before / curvature_sum)[None, None, :, None]
    new_residual = res_m - step_size * applied
    norm_after = lax.psum(sample_sums(new_residual * new_residual), ("order", "lat"))
    ratio_new = (norm_after / norm_before)[None, None, :, None]
    new_position = pos_m + step_size * dir_m
    new_direction = new_residual + ratio_new * dir_m
    return (new_position, new_residual, new_direction)


def solution(mesh):
    return jax.shard_map(
        shards,
        mesh=mesh,
        in_specs=(
            P("order", None, None, "lat"),
            P("order", None, None, "lat"),
            P("order", None, None, "lat"),
            P("order", None, "lat"),
            P(),
            P(("lat", "order"), None),
            P(("lat", "order"), None),
            P(),
            P("lat"),
        ),
        out_specs=(
            P("order", None, None, "lat"),
            P("order", None, None, "lat"),
            P("order", None, None, "lat"),
        ),
        check_vma=False,
    )
```

profile of v0, /device:TPU:1, one launch (start us, length us, event | category | flops | bytes accessed | tf_op | source)
XLA Modules:
  0.0 419.9 jit_solution(14200132624685688203)
XLA Ops:
  7.2 0.0 copy-start
  7.2 0.0 all-gather.2.cloned.1.call-start
  7.2 2.3 copy.20
  9.6 0.0 all-gather.2.cloned.1.call-update
  9.6 0.1 dynamic_slice.6
  9.7 0.7 fusion.11
  10.4 0.1 fusion.30
  10.6 0.9 fusion.37
  11.4 9.9 %fusion.17 = (f32[1,128,4320]{1,2,0:T(8,128)S(1)}, f32[1,128,4320]{1,2,0:T(8,128)}) fusion(s32[128]{0:T(128)S(1)} %copy-done.10), kind=kLoop, calls=%fused_computation.23 | loop fusion | flops 4976640 | bytes 4424192 | tf_op jit(solution)/shard_map/cos | solution.py:12
  21.3 44.9 %all-gather.2.cloned.1.call-done = f32[2,2,64,2160]{2,1,0,3:T(2,128)} async-done(((f32[2,2,64,540]{2,1,0,3:T(2,128)}), f32[2,2,64,2160]{2,1,0,3:T(2,128)}) %all-gather.2.cloned.1.call-update) | async-done | bytes 2211856 | tf_op jit(solution)/shard_map/all_gather | solution.py:37
  66.2 6.6 %broadcast_multiply_fusion = f32[2,2,64,2160]{2,1,0,3:T(2,128)S(1)} fusion(f32[2,2,64,2160]{2,1,0,3:T(2,128)} %all-gather.2.cloned.1.call-done, f32[2,2160]{0,1:T(8,128)S(1)} %fusion.30), kind=kLoop, calls=%fused_computation.18 | loop fusion | flops 552960 | bytes 4440960 | tf_op jit(solution)/shard_map/mul | solution.py:41
  72.8 8.7 %fusion.4 = f32[2,2,64,512]{3,2,1,0:T(8,128)S(1)} fusion(f32[2,2160,512]{2,1,0:T(8,128)S(1)} %copy-done.1, f32[2,2,64,2160]{2,1,0,3:T(2,128)S(1)} %broadcast_multiply_fusion), kind=kOutput, calls=%fused_computation.5 | convolution fusion | flops 3397386240 | bytes 11583488 | tf_op jit(solution)/shard_map/mskd,mdt->mtsk/dot_general | solution.py:42
  81.5 1.0 copy.22
  82.5 10.8 %all-to-all-start = ((f32[2,512,128]{2,0,1:T(2,128)}), f32[2,512,128]{2,0,1:T(2,128)S(1)}, u32[]{:S(2)}, u32[]{:S(2)}) async-start(f32[2,512,128]{2,0,1:T(2,128)} %copy.22), calls=%async_computation | async-start | bytes 1048576 | tf_op jit(solution)/shard_map/all_to_all | solution.py:43
  93.3 0.2 all-reduce.3.cloned.1.call-start
  93.6 17.4 %all-to-all-done = f32[2,512,128]{2,0,1:T(2,128)S(1)} async-done(((f32[2,512,128]{2,0,1:T(2,128)}), f32[2,512,128]{2,0,1:T(2,128)S(1)}, u32[]{:S(2)}, u32[]{:S(2)}) %all-to-all-start) | async-done | bytes 524320 | tf_op jit(solution)/shard_map/all_to_all | solution.py:43
  111.0 0.8 copy.24
  111.9 1.6 reshape.148
  113.5 31.3 %fusion.8 = f32[8,64,4320,1]{2,1,3,0:T(8,128)S(1)} fusion(f32[1,128,4320]{1,2,0:T(8,128)} %get-tuple-element.13, f32[1,128,4320]{1,2,0:T(8,128)S(1)} %get-tuple-element.12, f32[128,8,2,64]{3,2,1,0:T(2,128)S(1)} %reshape.148), kind=kOutput, calls=%fused_computation.10 | convolution fusion | flops 6795878400 | bytes 13795328 | tf_op jit(solution)/shard_map/mrsk,sml->rkl/dot_general | solution.py:55
  144.8 7.8 %fusion.24 = f32[128,8,2,64]{0,3,1,2:T(8,128)S(1)} fusion(f32[8,64,4320,1]{2,1,3,0:T(8,128)S(1)} %fusion.8, f32[8,4320]{1,0:T(8,128)S(1)} %fusion.33, f32[1,128,4320]{1,2,0:T(8,128)S(1)} %copy-done.2, f32[1,128,4320]{1,2,0:T(8,128)S(1)} %get-tuple-element.12), kind=kOutput, calls=%fused_computation.26 | convolution fusion | flops 6798221312 | bytes 13933568 | tf_op jit(solution)/shard_map/rkl,sml->mrsk/dot_general | solution.py:63
  152.7 0.2 copy.28
  153.0 23.3 %all_to_all.30 = f32[128,8,128]{2,1,0:T(8,128)S(1)} all-to-all(f32[128,8,128]{2,1,0:T(8,128)S(1)} %copy.28), channel_id=1, replica_groups=mesh['order'=64,'lat'=4] {'order'}, dimensions={0} | all-to-all | bytes 1048576 | tf_op jit(solution)/shard_map/all_to_all | solution.py:66
  176.3 0.6 reshape.150
  176.9 19.2 %fusion.2 = f32[2,2,64,2160]{3,2,1,0:T(8,128)} fusion(f32[2,2160,512]{2,1,0:T(8,128)} %param.12, f32[2,512,2,64]{3,2,1,0:T(2,128)S(1)} %reshape.150), kind=kOutput, calls=%fused_computation.3 | convolution fusion | flops 3397386240 | bytes 11583488 | tf_op jit(solution)/shard_map/mtsk,mdt->mskd/dot_general | solution.py:74
  196.2 0.0 all-reduce.3.cloned.1.call-update
  196.2 0.1 compare_convert_fusion
  196.3 61.3 %all-reduce.3.cloned.1.call-done = f32[2,2,64,2160]{3,2,1,0:T(8,128)} async-done(((f32[2,2,64,2160]{3,2,1,0:T(8,128)}), f32[2,2,64,2160]{3,2,1,0:T(8,128)}) %all-reduce.3.cloned.1.call-update) | async-done | bytes 2211856 | tf_op jit(solution)/shard_map/psum | solution.py:75
  257.6 1.6 multiply_reduce_fusion.1
  259.2 76.0 %all-reduce = (f32[64]{0:T(128)S(1)}, f32[64]{0:T(128)S(1)}) all-reduce(f32[64]{0:T(128)S(1)} %get-tuple-element.4, f32[64]{0:T(128)S(1)} %get-tuple-element.3), channel_id=1, replica_groups=mesh['order'=64,'lat'=4] {'order','lat'}, use_global_device_ids=true, to_apply=%region_1.0 | all-reduce | flops 128 | bytes 1024 | tf_op jit(solution)/shard_map/psum | solution.py:36
  335.1 2.5 multiply_reduce_fusion
  337.6 74.3 %psum.31 = f32[64]{0:T(128)S(1)} all-reduce(f32[64]{0:T(128)S(1)} %get-tuple-element.7), channel_id=1, replica_groups=mesh['order'=64,'lat'=4] {'order','lat'}, use_global_device_ids=true, to_apply=%region_6.7 | all-reduce | flops 64 | bytes 512 | tf_op jit(solution)/shard_map/psum | solution.py:81
  411.9 1.0 multiply_add_fusion
  (30 shorter events, 0.2 us)
Async XLA Ops:
  7.2 2.5 copy-start
  7.2 2.4 copy-start.10
  7.2 2.5 copy-start.11
  7.2 59.0 %all-gather.2.cloned.1.call-start = ((), (), s32[]{:S(2)}) async-start(), calls=%async_computation.2 | async-start | bytes 5529600 | tf_op jit(solution)/shard_map/all_gather | solution.py:37
  66.2 6.6 %copy-start.1 = (f32[2,2160,512]{2,1,0:T(8,128)S(1)}, f32[2,2160,512]{2,1,0:T(8,128)}, u32[]{:S(2)}) copy-start(f32[2,2160,512]{2,1,0:T(8,128)} %param.12) | copy-start | bytes 26542084
  72.7 20.8 %copy-start.7 = (f32[8,4320,1]{1,2,0:T(1,128)S(1)}, f32[8,4320,1]{1,2,0:T(1,128)}, u32[]{:S(2)}) copy-start(f32[8,4320,1]{1,2,0:T(1,128)} %get-tuple-element.11) | copy-start | bytes 414724
  72.8 20.8 %copy-start.8 = (s32[8,4320]{1,0:T(8,128)S(1)}, s32[8,4320]{1,0:T(8,128)}, u32[]{:S(2)}) copy-start(s32[8,4320]{1,0:T(8,128)} %param.15) | copy-start | bytes 414724
  82.5 28.5 %all-to-all-start = ((f32[2,512,128]{2,0,1:T(2,128)}), f32[2,512,128]{2,0,1:T(2,128)S(1)}, u32[]{:S(2)}, u32[]{:S(2)}) async-start(f32[2,512,128]{2,0,1:T(2,128)} %copy.22), calls=%async_computation | async-start | bytes 1048576 | tf_op jit(solution)/shard_map/all_to_all | solution.py:43
  93.3 164.3 %all-reduce.3.cloned.1.call-start = ((), (), s32[]{:S(2)}) async-start(), calls=%async_computation.3 | async-start | bytes 4456448 | tf_op jit(solution)/shard_map/psum | solution.py:75
  113.5 31.3 %copy-start.2 = (f32[1,128,4320]{1,2,0:T(8,128)S(1)}, f32[1,128,4320]{1,2,0:T(8,128)}, u32[]{:S(2)}) copy-start(f32[1,128,4320]{1,2,0:T(8,128)} %get-tuple-element.13) | copy-start | bytes 6635524
  196.2 61.4 %copy-start.3 = (f32[2,2,64,540]{3,2,1,0:T(8,128)S(1)}, f32[2,2,64,540]{3,2,1,0:T(8,128)}, u32[]{:S(2)}) copy-start(f32[2,2,64,540]{3,2,1,0:T(8,128)} %param.11) | copy-start | bytes 1658884
  196.2 61.4 %copy-start.4 = (f32[2,2,64,540]{3,2,1,0:T(8,128)S(1)}, f32[2,2,64,540]{3,2,1,0:T(8,128)}, u32[]{:S(2)}) copy-start(f32[2,2,64,540]{3,2,1,0:T(8,128)} %param.10) | copy-start | bytes 1658884
  196.2 61.4 %copy-start.9 = (f32[540]{0:T(1024)S(1)}, f32[540]{0:T(1024)}, u32[]{:S(2)}) copy-start(f32[540]{0:T(1024)} %param.17) | copy-start | bytes 6484
  196.2 138.9 %copy-start.6 = (f32[2,2,64,540]{3,2,1,0:T(8,128)S(1)}, f32[2,2,64,540]{3,2,1,0:T(8,128)}, u32[]{:S(2)}) copy-start(f32[2,2,64,540]{3,2,1,0:T(8,128)} %param.9) | copy-start | bytes 1658884
  337.6 75.3 %copy-start.5 = (f32[2,2,64,540]{3,2,1,0:T(8,128)}, f32[2,2,64,540]{3,2,1,0:T(8,128)S(1)}, u32[]{:S(2)}) copy-start(f32[2,2,64,540]{3,2,1,0:T(8,128)S(1)} %get-tuple-element.8) | copy-start | bytes 1658884
Sparse Core Ops, SparseCore 0:
  9.8 56.2 all-gather.1
  196.3 61.1 all-reduce.2
where the time goes:
time: 429 us; the launch traced here: 420 us
  blocking collectives  174 us (41%)
  waiting for transfers between devices  124 us (29%)
  matrix products  67.8 us (16%)
  other arithmetic  21.7 us (5%)
  between operations  14.5 us (3%)
  starting transfers between devices  11.1 us (3%)
  local copies, waits for them, and re-layouts  7.76 us (2%)
    psum x1, blocking collectives, shards(): norm_before = lax.psum(sample_sums(res_m * res_m), ('order', 'lat'))  76 us
    psum x1, blocking collectives, shards(): lax.psum(sample_sums(new_residual * new_residual), ('order', 'lat'))  74.3 us
    psum x1, waiting for transfers between devices, shards(): totals = lax.psum(band_part, 'lat')  61.3 us
    all_gather x1, waiting for transfers between devices, shards(): block_part = lax.all_gather(direction, 'lat', axis=3, tiled=True)  44.9 us
    dot_general x1, matrix products, shards(): surface = jnp.einsum('mrsk,sml->rkl', grid_in, harmonic, precision=highest)  31.3 us
    all_to_all x1, blocking collectives, shards(): lax.all_to_all(spectra.reshape(orders_all, rows_here, 2 * samples), 'orde...  23.3 us
    dot_general x1, matrix products, shards(): jnp.einsum('mtsk,mdt->mskd', returned, legendre, precision=highest)  19.2 us
    all_to_all x1, waiting for transfers between devices, shards(): lax.all_to_all(synthesis.reshape(m_local, band_rows, 2 * samples), 'order...  17.4 us
  transfers between devices with their start and end apart: 3, of which 3 were waited for; matrix products, arithmetic and copies ran while one was open for 3% of the time, Pallas kernels for 0%

commit v1 on v0

--- a/solution.py
+++ b/solution.py
@@ -3,6 +3,15 @@
 import jax.numpy as jnp
 from jax import lax
 from jax.sharding import PartitionSpec as P
+
+
+def turn_the_roots(raw, axis_name):
+    p_count = lax.axis_size(axis_name)
+    piece_out = lambda z1: [(k, k ^ z1) for k in range(p_count)]
+    w2 = raw
+    for to_i in range(p_count.bit_length() - 1):
+        w2 = w2 + lax.ppermute(w2, axis_name, piece_out(1 << to_i))
+    return w2
 
 
 def tables(order_of, longitudes):
@@ -72,7 +81,7 @@
     )
     returned = returned.reshape(m_local, band_rows, 2, samples)
     band_part = jnp.einsum("mtsk,mdt->mskd", returned, legendre, precision=highest)
-    totals = lax.psum(band_part, "lat")
+    totals = turn_the_roots(band_part, "lat")
     summed = lax.dynamic_slice_in_dim(totals, deg_start, deg_local, 3)
     applied = (summed + damping[None, None, None, :] * dir_m) * own_valid
     curvature_sum = lax.psum(sample_sums(dir_m * applied), ("order", "lat"))

time: 429 us -> 467 us (1.089)
  waiting for transfers between devices: 124 us -> 159 us
    ppermute x0 -> x2, waiting for transfers between devices: none -> 96.8 us  [turn_the_roots(): w2 = w2 + lax.ppermute(w2, axis_name, piece_out(1 << to_i))]
    psum x1 -> x0, waiting for transfers between devices: 61.3 us -> none  [shards(): totals = lax.psum(band_part, 'lat')]
  transfers between devices with their start and end apart: 3 -> 4, of which waited for: 3 -> 4; matrix products, arithmetic and copies ran while one was open for 3% -> 3% of each run, Pallas kernels for 0% -> 0%
where the time goes in v1:
time: 467 us; the launch traced here: 458 us
  blocking collectives  171 us (37%)
  waiting for transfers between devices  159 us (34%)
  matrix products  66.6 us (14%)
  other arithmetic  24.8 us (5%)
  between operations  14.5 us (3%)
  starting transfers between devices  13.6 us (3%)
  local copies, waits for them, and re-layouts  8.27 us (2%)
    ppermute x2, waiting for transfers between devices, turn_the_roots(): w2 = w2 + lax.ppermute(w2, axis_name, piece_out(1 << to_i))  96.8 us
    psum x1, blocking collectives, shards(): norm_before = lax.psum(sample_sums(res_m * res_m), ('order', 'lat'))  74.4 us
    psum x1, blocking collectives, shards(): lax.psum(sample_sums(new_residual * new_residual), ('order', 'lat'))  73.3 us
    all_gather x1, waiting for transfers between devices, shards(): block_part = lax.all_gather(direction, 'lat', axis=3, tiled=True)  44.9 us
    dot_general x1, matrix products, shards(): surface = jnp.einsum('mrsk,sml->rkl', grid_in, harmonic, precision=highest)  31.3 us
    all_to_all x1, blocking collectives, shards(): lax.all_to_all(spectra.reshape(orders_all, rows_here, 2 * samples), 'orde...  23.3 us
    dot_general x1, matrix products, shards(): jnp.einsum('mtsk,mdt->mskd', returned, legendre, precision=highest)  18.1 us
    all_to_all x1, waiting for transfers between devices, shards(): lax.all_to_all(synthesis.reshape(m_local, band_rows, 2 * samples), 'order...  17.5 us
  transfers between devices with their start and end apart: 4, of which 4 were waited for; matrix products, arithmetic and copies ran while one was open for 3% of the time, Pallas kernels for 0%

profile of v1, /device:TPU:1, one launch (start us, length us, event | category | flops | bytes accessed | tf_op | source)
XLA Modules:
  0.0 457.9 jit_solution(4965045944011876179)
XLA Ops:
  7.2 2.3 copy.20
  9.7 0.7 fusion.11
  10.4 0.1 fusion.30
  10.6 0.9 fusion.39
  11.4 9.8 %fusion.17 = (f32[1,128,4320]{1,2,0:T(8,128)S(1)}, f32[1,128,4320]{1,2,0:T(8,128)}) fusion(s32[128]{0:T(128)S(1)} %copy-done.10), kind=kLoop, calls=%fused_computation.23 | loop fusion | flops 4976640 | bytes 4424192 | tf_op jit(solution)/shard_map/cos | solution.py:21
  21.3 44.9 %all-gather.2.cloned.1.call-done = f32[2,2,64,2160]{2,1,0,3:T(2,128)} async-done(((f32[2,2,64,540]{2,1,0,3:T(2,128)}), f32[2,2,64,2160]{2,1,0,3:T(2,128)}) %all-gather.2.cloned.1.call-update) | async-done | bytes 2211856 | tf_op jit(solution)/shard_map/all_gather | solution.py:46
  66.2 6.6 %broadcast_multiply_fusion = f32[2,2,64,2160]{2,1,0,3:T(2,128)S(1)} fusion(f32[2,2,64,2160]{2,1,0,3:T(2,128)} %all-gather.2.cloned.1.call-done, f32[2,2160]{0,1:T(8,128)S(1)} %fusion.30), kind=kLoop, calls=%fused_computation.18 | loop fusion | flops 552960 | bytes 4440960 | tf_op jit(solution)/shard_map/mul | solution.py:50
  72.8 8.7 %fusion.4 = f32[2,2,64,512]{3,2,1,0:T(8,128)S(1)} fusion(f32[2,2160,512]{2,1,0:T(8,128)S(1)} %copy-done.1, f32[2,2,64,2160]{2,1,0,3:T(2,128)S(1)} %broadcast_multiply_fusion), kind=kOutput, calls=%fused_computation.5 | convolution fusion | flops 3397386240 | bytes 11583488 | tf_op jit(solution)/shard_map/mskd,mdt->mtsk/dot_general | solution.py:51
  81.5 1.0 copy.22
  82.5 11.0 %all-to-all-start = ((f32[2,512,128]{2,0,1:T(2,128)}), f32[2,512,128]{2,0,1:T(2,128)S(1)}, u32[]{:S(2)}, u32[]{:S(2)}) async-start(f32[2,512,128]{2,0,1:T(2,128)} %copy.22), calls=%async_computation | async-start | bytes 1048576 | tf_op jit(solution)/shard_map/all_to_all | solution.py:52
  93.5 17.5 %all-to-all-done = f32[2,512,128]{2,0,1:T(2,128)S(1)} async-done(((f32[2,512,128]{2,0,1:T(2,128)}), f32[2,512,128]{2,0,1:T(2,128)S(1)}, u32[]{:S(2)}, u32[]{:S(2)}) %all-to-all-start) | async-done | bytes 524320 | tf_op jit(solution)/shard_map/all_to_all | solution.py:52
  111.0 0.8 copy.24
  111.9 1.6 reshape.148
  113.5 31.3 %fusion.8 = f32[8,64,4320,1]{2,1,3,0:T(8,128)S(1)} fusion(f32[1,128,4320]{1,2,0:T(8,128)} %get-tuple-element.13, f32[1,128,4320]{1,2,0:T(8,128)S(1)} %get-tuple-element.12, f32[128,8,2,64]{3,2,1,0:T(2,128)S(1)} %reshape.148), kind=kOutput, calls=%fused_computation.10 | convolution fusion | flops 6795878400 | bytes 13795328 | tf_op jit(solution)/shard_map/mrsk,sml->rkl/dot_general | solution.py:64
  144.8 7.8 %fusion.24 = f32[128,8,2,64]{0,3,1,2:T(8,128)S(1)} fusion(f32[8,64,4320,1]{2,1,3,0:T(8,128)S(1)} %fusion.8, f32[8,4320]{1,0:T(8,128)S(1)} %fusion.35, f32[1,128,4320]{1,2,0:T(8,128)S(1)} %copy-done.2, f32[1,128,4320]{1,2,0:T(8,128)S(1)} %get-tuple-element.12), kind=kOutput, calls=%fused_computation.26 | convolution fusion | flops 6798221312 | bytes 13933568 | tf_op jit(solution)/shard_map/rkl,sml->mrsk/dot_general | solution.py:72
  152.7 0.2 copy.28
  153.0 23.3 %all_to_all.30 = f32[128,8,128]{2,1,0:T(8,128)S(1)} all-to-all(f32[128,8,128]{2,1,0:T(8,128)S(1)} %copy.28), channel_id=1, replica_groups=mesh['order'=64,'lat'=4] {'order'}, dimensions={0} | all-to-all | bytes 1048576 | tf_op jit(solution)/shard_map/all_to_all | solution.py:75
  176.3 0.6 reshape.150
  176.9 18.1 %fusion.2 = f32[2,2,64,2160]{3,2,1,0:T(8,128)S(1)} fusion(f32[2,2160,512]{2,1,0:T(8,128)} %param.12, f32[2,512,2,64]{3,2,1,0:T(2,128)S(1)} %reshape.150), kind=kOutput, calls=%fused_computation.3 | convolution fusion | flops 3397386240 | bytes 11583488 | tf_op jit(solution)/shard_map/mtsk,mdt->mskd/dot_general | solution.py:83
  195.1 0.7 collective-permute-start
  195.7 49.0 %collective-permute-done = f32[2,2,64,2160]{3,2,1,0:T(8,128)S(1)} collective-permute-done((f32[2,2,64,2160]{3,2,1,0:T(8,128)S(1)}, f32[2,2,64,2160]{3,2,1,0:T(8,128)S(1)}, u32[]{:S(2)}, u32[]{:S(2)}) %collective-permute-start) | collective-permute-done | bytes 2211872 | tf_op jit(solution)/shard_map/ppermute | solution.py:13
  244.8 0.3 add.58
  245.1 1.9 collective-permute-start.1
  247.0 0.7 compare_convert_fusion
  247.7 47.8 %collective-permute-done.1 = f32[2,2,64,2160]{3,2,1,0:T(8,128)} collective-permute-done((f32[2,2,64,2160]{3,2,1,0:T(8,128)S(1)}, f32[2,2,64,2160]{3,2,1,0:T(8,128)}, u32[]{:S(2)}, u32[]{:S(2)}) %collective-permute-start.1) | collective-permute-done | bytes 2211872 | tf_op jit(solution)/shard_map/ppermute | solution.py:13
  295.5 2.2 multiply_reduce_fusion.1
  297.8 74.4 %all-reduce = (f32[64]{0:T(128)S(1)}, f32[64]{0:T(128)S(1)}) all-reduce(f32[64]{0:T(128)} %get-tuple-element.4, f32[64]{0:T(128)} %get-tuple-element.3), channel_id=1, replica_groups=mesh['order'=64,'lat'=4] {'order','lat'}, use_global_device_ids=true, to_apply=%region_1.0 | all-reduce | flops 128 | bytes 1024 | tf_op jit(solution)/shard_map/psum | solution.py:45
  372.2 0.5 copy-done.12
  372.7 3.3 multiply_reduce_fusion
  376.0 73.3 %psum.23 = f32[64]{0:T(128)S(1)} all-reduce(f32[64]{0:T(128)} %get-tuple-element.7), channel_id=1, replica_groups=mesh['order'=64,'lat'=4] {'order','lat'}, use_global_device_ids=true, to_apply=%region_5.6 | all-reduce | flops 64 | bytes 512 | tf_op jit(solution)/shard_map/psum | solution.py:90
  449.3 0.6 div.7
  449.9 1.0 multiply_add_fusion
  (34 shorter events, 0.3 us)
Async XLA Ops:
  7.2 2.5 copy-start
  7.2 2.4 copy-start.10
  7.2 2.5 copy-start.11
  7.2 59.0 %all-gather.2.cloned.1.call-start = ((), (), s32[]{:S(2)}) async-start(), calls=%async_computation.2 | async-start | bytes 5529600 | tf_op jit(solution)/shard_map/all_gather | solution.py:46
  9.7 1.7 copy-start.9
  66.2 6.6 %copy-start.1 = (f32[2,2160,512]{2,1,0:T(8,128)S(1)}, f32[2,2160,512]{2,1,0:T(8,128)}, u32[]{:S(2)}) copy-start(f32[2,2160,512]{2,1,0:T(8,128)} %param.12) | copy-start | bytes 26542084
  72.7 20.7 %copy-start.6 = (f32[8,4320,1]{1,2,0:T(1,128)S(1)}, f32[8,4320,1]{1,2,0:T(1,128)}, u32[]{:S(2)}) copy-start(f32[8,4320,1]{1,2,0:T(1,128)} %get-tuple-element.11) | copy-start | bytes 414724
  72.8 20.7 %copy-start.7 = (s32[8,4320]{1,0:T(8,128)S(1)}, s32[8,4320]{1,0:T(8,128)}, u32[]{:S(2)}) copy-start(s32[8,4320]{1,0:T(8,128)} %param.15) | copy-start | bytes 414724
  82.5 28.5 %all-to-all-start = ((f32[2,512,128]{2,0,1:T(2,128)}), f32[2,512,128]{2,0,1:T(2,128)S(1)}, u32[]{:S(2)}, u32[]{:S(2)}) async-start(f32[2,512,128]{2,0,1:T(2,128)} %copy.22), calls=%async_computation | async-start | bytes 1048576 | tf_op jit(solution)/shard_map/all_to_all | solution.py:52
  113.5 31.3 %copy-start.2 = (f32[1,128,4320]{1,2,0:T(8,128)S(1)}, f32[1,128,4320]{1,2,0:T(8,128)}, u32[]{:S(2)}) copy-start(f32[1,128,4320]{1,2,0:T(8,128)} %get-tuple-element.13) | copy-start | bytes 6635524
  195.0 100.5 %copy-start.3 = (f32[2,2,64,540]{3,2,1,0:T(8,128)S(1)}, f32[2,2,64,540]{3,2,1,0:T(8,128)}, u32[]{:S(2)}) copy-start(f32[2,2,64,540]{3,2,1,0:T(8,128)} %param.11) | copy-start | bytes 1658884
  195.0 100.5 %copy-start.5 = (f32[2,2,64,540]{3,2,1,0:T(8,128)S(1)}, f32[2,2,64,540]{3,2,1,0:T(8,128)}, u32[]{:S(2)}) copy-start(f32[2,2,64,540]{3,2,1,0:T(8,128)} %param.10) | copy-start | bytes 1658884
  195.0 100.5 %copy-start.8 = (f32[540]{0:T(1024)S(1)}, f32[540]{0:T(1024)}, u32[]{:S(2)}) copy-start(f32[540]{0:T(1024)} %param.17) | copy-start | bytes 6484
  195.1 49.7 %collective-permute-start = (f32[2,2,64,2160]{3,2,1,0:T(8,128)S(1)}, f32[2,2,64,2160]{3,2,1,0:T(8,128)S(1)}, u32[]{:S(2)}, u32[]{:S(2)}) collective-permute-start(f32[2,2,64,2160]{3,2,1,0:T(8,128)S(1)} %fusion.2), channel_id=1, source_target_pairs={{0,1},{1,0},{2,3},{3,2},{4,5},{5,4},{6,7},{7,6},{8,9},{9,8},{10,11... | collective-permute-start | bytes 6635528 | tf_op jit(solution)/shard_map/ppermute | solution.py:13
  245.1 50.4 %collective-permute-start.1 = (f32[2,2,64,2160]{3,2,1,0:T(8,128)S(1)}, f32[2,2,64,2160]{3,2,1,0:T(8,128)}, u32[]{:S(2)}, u32[]{:S(2)}) collective-permute-start(f32[2,2,64,2160]{3,2,1,0:T(8,128)S(1)} %add.58), channel_id=1, source_target_pairs={{0,2},{1,3},{2,0},{3,1},{4,6},{5,7},{6,4},{7,5},{8,10},{9,11},{10,... | collective-permute-start | bytes 6635528 | tf_op jit(solution)/shard_map/ppermute | solution.py:13
  372.2 0.5 copy-start.12
  376.0 74.9 %copy-start.4 = (f32[2,2,64,540]{3,2,1,0:T(8,128)}, f32[2,2,64,540]{3,2,1,0:T(8,128)S(1)}, u32[]{:S(2)}) copy-start(f32[2,2,64,540]{3,2,1,0:T(8,128)S(1)} %get-tuple-element.8) | copy-start | bytes 1658884
Sparse Core Ops, SparseCore 0:
  9.8 56.2 all-gather.1
